TPU v7x, 512 devices: a whole 4x8x8 slice. The times are simulated.
512 devices in a mesh: vocab: 64 (over y, z_hi, core), width: 8 (over z_lo, x).
Axes of the slice: x: 4, y: 8, z: 8 (z_hi: 4, z_lo: 2; z = z_hi * 2 + z_lo), core: 2. Of those that a mesh axis runs over, the one named last changes fastest.
Arguments:
- head_weight: bfloat16 [4096, 65536], P('width', 'vocab'), may hold values from -3 to 3
- direction: bfloat16 [4096, 65536], P('width', 'vocab'), may hold values from -150 to 150
- residual: bfloat16 [4096, 65536], P('width', 'vocab'), may hold values from -150 to 150
- hidden: bfloat16 [512, 4096], P('vocab', 'width'), may hold values from -200 to 200
- fold_ids: int32 [512], replicated, may hold values from 0 to 7
Outputs:
- new_direction: bfloat16 [4096, 65536], P('width', 'vocab')
All inputs are finite; a program needn't handle non-finite values.
Results may differ from a plain program's by a relative error of at most 0.0085.
Values may be sent and summed in bfloat16 or wider, within the bound.
A program may use at most 64 MiB of HBM per device.

v0:
```python
import jax
import jax.numpy as jnp
from jax import lax
from jax.sharding import PartitionSpec as P

DAMPING = 0.02
CONTRACT_LEAD = (((0,), (1,)), ((), ()))


def local(head_weight, direction, residual, hidden, fold_ids):
    wide_panel = lax.all_gather(hidden, "width", axis=1, tiled=True)
    panels = lax.all_gather(wide_panel, "vocab", axis=0, tiled=True)
    weight_cols, direction_cols = (
        lax.all_to_all(head_weight, "width", split_axis=1, concat_axis=0, tiled=True),
        lax.all_to_all(direction, "width", split_axis=1, concat_axis=0, tiled=True),
    )
    logit_rows = lax.dot_general(
        weight_cols, panels, CONTRACT_LEAD, preferred_element_type=jnp.float32
    )
    tangent_rows = lax.dot_general(
        direction_cols, panels, CONTRACT_LEAD, preferred_element_type=jnp.float32
    )
    local_top = jnp.max(logit_rows, axis=0)
    row_top = lax.pmax(local_top, ("vocab", "width"))
    weights = jnp.exp(logit_rows - row_top[None, :])
    row_total, row_moment = lax.psum(
        (jnp.sum(weights, axis=0), jnp.sum(weights * tangent_rows, axis=0)), ("vocab", "width")
    )
    kept_mask = (fold_ids != 0).astype(jnp.float32)
    row_mean = row_moment / row_total
    curving = (
        kept_mask[None, :] * (weights / row_total[None, :]) * (tangent_rows - row_mean[None, :])
    ).astype(jnp.bfloat16)
    column_block = lax.dot_general(
        panels, curving, CONTRACT_LEAD, preferred_element_type=jnp.float32
    )
    curvature = lax.all_to_all(column_block, "width", split_axis=0, concat_axis=1, tiled=True)
    direction_wide = direction.astype(jnp.float32)
    residual_wide = residual.astype(jnp.float32)
    operator_image = curvature + DAMPING * direction_wide
    squares, curvature_sum = lax.psum(
        (jnp.sum(residual_wide * residual_wide), jnp.sum(direction_wide * operator_image)),
        ("vocab", "width"),
    )
    step_size = squares / curvature_sum
    moved = residual_wide - step_size * operator_image
    next_squares = lax.psum(jnp.sum(moved * moved), ("vocab", "width"))
    mixing = next_squares / squares
    return (moved + mixing * direction_wide).astype(jnp.bfloat16)


def solution(mesh):
    placed = (
        P("width", "vocab"),
        P("width", "vocab"),
        P("width", "vocab"),
        P("vocab", "width"),
        P(),
    )
    return jax.shard_map(
        local, mesh=mesh, in_specs=placed, out_specs=P("width", "vocab"), check_vma=False
    )
```

profile of v0, /device:TPU:1, one launch (start us, length us, event | category | flops | bytes accessed | tf_op | source)
XLA Modules:
  0.0 570.6 jit_solution(6129876579250119001)
XLA Ops:
  6.5 0.0 all-gather.2.cloned.1.call-start
  6.5 26.3 %all_gather.6 = bf16[8,4096]{1,0:T(8,128)(2,1)} all-gather(bf16[8,512]{1,0:T(8,128)(2,1)} %param.8), channel_id=1, replica_groups=mesh['vocab'=64,'width'=8] {'width'}, dimensions={1}, use_global_device_ids=true | all-gather | bytes 73728 | tf_op jit(solution)/shard_map/all_gather | solution.py:11
  32.8 0.0 all-gather.2.cloned.1.call-update
  32.8 0.0 copy-start
  32.9 2.4 copy.13
  35.2 4.1 all-to-all-start
  39.3 0.0 copy-done
  39.3 0.0 copy-start.1
  39.4 1.3 copy.15
  40.7 8.1 %all-to-all-done = bf16[512,8,128]{0,2,1:T(8,128)(2,1)S(1)} async-done(((bf16[512,8,128]{0,2,1:T(8,128)(2,1)}), bf16[512,8,128]{0,2,1:T(8,128)(2,1)S(1)}, u32[]{:S(2)}, u32[]{:S(2)}) %all-to-all-start) | async-done | bytes 1048608 | tf_op jit(solution)/shard_map/all_to_all | solution.py:14
  48.8 4.2 all-to-all-start.1
  53.0 0.0 copy-done.1
  53.1 0.7 copy.14
  53.7 11.8 %all-to-all-done.1 = bf16[512,8,128]{0,2,1:T(8,128)(2,1)} async-done(((bf16[512,8,128]{0,2,1:T(8,128)(2,1)}), bf16[512,8,128]{0,2,1:T(8,128)(2,1)}, u32[]{:S(2)}, u32[]{:S(2)}) %all-to-all-start.1) | async-done | bytes 1048608 | tf_op jit(solution)/shard_map/all_to_all | solution.py:15
  65.5 1.6 copy.16
  67.2 64.0 %all-gather.2.cloned.1.call-done = bf16[512,4096]{1,0:T(8,128)(2,1)} async-done(((bf16[8,4096]{1,0:T(8,128)(2,1)}), bf16[512,4096]{1,0:T(8,128)(2,1)}) %all-gather.2.cloned.1.call-update) | async-done | bytes 4194320 | tf_op jit(solution)/shard_map/all_gather | solution.py:12
  131.1 3.7 fusion.11
  134.8 96.2 %pmax.7 = f32[512]{0:T(512)S(1)} all-reduce(f32[512]{0:T(512)S(1)} %get-tuple-element.11), channel_id=1, replica_groups=mesh['vocab'=64,'width'=8] {'vocab','width'}, use_global_device_ids=true, to_apply=%region_3.0 | all-reduce | flops 512 | bytes 4096 | tf_op jit(solution)/shard_map/pmax | solution.py:24
  231.0 3.7 fusion.5
  234.7 93.4 %all-reduce.1 = (f32[512]{0:T(512)S(1)}, f32[512]{0:T(512)S(1)}) all-reduce(f32[512]{0:T(512)S(1)} %get-tuple-element.6, f32[512]{0:T(512)S(1)} %get-tuple-element.5), channel_id=1, replica_groups=mesh['vocab'=64,'width'=8] {'vocab','width'}, use_global_device_ids=true, to_apply=%region_7.0 | all-reduce | flops 1024 | bytes 8192 | tf_op jit(solution)/shard_map/psum | solution.py:26
  328.1 2.9 fusion.6
  331.1 0.2 copy.21
  331.3 29.6 %all_to_all.57 = f32[8,512,128]{1,2,0:T(8,128)} all-to-all(f32[8,512,128]{1,2,0:T(8,128)S(1)} %bitcast.19), channel_id=1, replica_groups=mesh['vocab'=64,'width'=8] {'width'}, dimensions={0} | all-to-all | bytes 4194304 | tf_op jit(solution)/shard_map/all_to_all | solution.py:37
  360.9 1.9 copy.18
  362.8 2.5 fusion
  365.3 95.9 %all-reduce = (f32[]{:T(128)}, f32[]{:T(128)}) all-reduce(f32[]{:T(128)} %get-tuple-element.14, f32[]{:T(128)} %get-tuple-element.15), channel_id=1, replica_groups=mesh['vocab'=64,'width'=8] {'vocab','width'}, use_global_device_ids=true, to_apply=%region_1.0 | all-reduce | flops 2 | bytes 16 | tf_op jit(solution)/shard_map/psum | solution.py:41
  462.4 2.5 multiply_reduce_fusion
  464.9 94.6 %psum.39 = f32[]{:T(128)} all-reduce(f32[]{:T(128)} %multiply_reduce_fusion), channel_id=1, replica_groups=mesh['vocab'=64,'width'=8] {'vocab','width'}, use_global_device_ids=true, to_apply=%region_11.0 | all-reduce | flops 1 | bytes 8 | tf_op jit(solution)/shard_map/psum | solution.py:47
  560.9 2.8 fusion.4
  (2 shorter events, 0.0 us)
Async XLA Ops:
  6.5 124.6 %all-gather.2.cloned.1.call-start = ((), (), s32[]{:S(2)}) async-start(), calls=%async_computation.3 | async-start | bytes 4259840 | tf_op jit(solution)/shard_map/all_gather | solution.py:12
  32.8 6.5 %copy-start = (bf16[512,1024]{1,0:T(8,128)(2,1)S(1)}, bf16[512,1024]{1,0:T(8,128)(2,1)}, u32[]{:S(2)}) copy-start(bf16[512,1024]{1,0:T(8,128)(2,1)} %param.6) | copy-start | bytes 3145732
  35.2 13.6 %all-to-all-start = ((bf16[512,8,128]{0,2,1:T(8,128)(2,1)}), bf16[512,8,128]{0,2,1:T(8,128)(2,1)S(1)}, u32[]{:S(2)}, u32[]{:S(2)}) async-start(bf16[512,8,128]{0,2,1:T(8,128)(2,1)} %bitcast), calls=%async_computation | async-start | bytes 2097152 | tf_op jit(solution)/shard_map/all_to_all | solution.py:14
  39.3 13.7 %copy-start.1 = (s32[512]{0:T(512)S(1)}, s32[512]{0:T(512)}, u32[]{:S(2)}) copy-start(s32[512]{0:T(512)} %param.9) | copy-start | bytes 6148
  48.8 16.8 %all-to-all-start.1 = ((bf16[512,8,128]{0,2,1:T(8,128)(2,1)}), bf16[512,8,128]{0,2,1:T(8,128)(2,1)}, u32[]{:S(2)}, u32[]{:S(2)}) async-start(bf16[512,8,128]{0,2,1:T(8,128)(2,1)} %bitcast.3), calls=%async_computation.1 | async-start | bytes 2097152 | tf_op jit(solution)/shard_map/all_to_all | solution.py:15
Sparse Core Ops, SparseCore 0:
  33.0 98.1 all-gather.1
where the time goes:
time: 571 us
  blocking collectives  436 us (76%)
  waiting for transfers between devices  83.9 us (15%)
  between operations  16.1 us (3%)
  matrix products  10.4 us (2%)
  starting transfers between devices  8.36 us (1%)
  local copies, waits for them, and re-layouts  8.15 us (1%)
  other arithmetic  7.74 us (1%)
    pmax x1, blocking collectives, local(): row_top = lax.pmax(local_top, ('vocab', 'width'))  96.2 us
    psum x1, blocking collectives, local(): lax.psum((jnp.sum(residual_wide * residual_wide), jnp.sum(direction_wide...  95.9 us
    psum x1, blocking collectives, local(): next_squares = lax.psum(jnp.sum(moved * moved), ('vocab', 'width'))  94.6 us
    psum x1, blocking collectives, local(): lax.psum((jnp.sum(weights, axis=0), jnp.sum(weights * tangent_rows, axis=...  93.4 us
    all_gather x1, waiting for transfers between devices, local(): panels = lax.all_gather(wide_panel, 'vocab', axis=0, tiled=True)  64 us
    all_to_all x1, blocking collectives, local(): lax.all_to_all(column_block, 'width', split_axis=0, concat_axis=1, tiled=...  29.6 us
    all_gather x1, blocking collectives, local(): wide_panel = lax.all_gather(hidden, 'width', axis=1, tiled=True)  26.3 us
    all_to_all x1, waiting for transfers between devices, local(): lax.all_to_all(direction, 'width', split_axis=1, concat_axis=0, tiled=True)  11.8 us
  transfers between devices with their start and end apart: 3, of which 3 were waited for; matrix products, arithmetic and copies ran while one was open for 1% of the time, Pallas kernels for 0%

commit v1 on v0

v1 whole, which is shorter than its diff:
```python
import jax
import jax.numpy as jnp
from jax import lax
from jax.experimental import pallas as pl
from jax.experimental.pallas import tpu as pltpu
from jax.sharding import PartitionSpec as P

DAMPING = 0.02
MESH = pl.DeviceIdType.MESH
NY, NZH, NC, NZL, NX = 8, 4, 2, 2, 4
F = 512
CW = 256


def kernel(
    head, dirn, res, hid, fold, out,
    hg, wb, dv, rv, img, cb, hown, ht, hsib, hblk, own, zs, zr,
    a1, a2, a3, b1, b2, b3,
    sib_s, sib_r, hx_s, hx_r, hz_s, hz_r, yr_s, yr_r, sb_s, sb_r,
    w_s, w_r, loc, z_s, z_r, cz_s, cz_r, cx_s, cx_r,
    a1_s, a1_r, a2_s, a2_r, a3_s, a3_r,
    b1_s, b1_r, b2_s, b2_r, b3_s, b3_r,
):
    f32, bf16 = jnp.float32, jnp.bfloat16
    hf = F // 2
    hl = NX * hf
    ch = CW // 2
    nb = NY * NZH
    nb2 = nb // 2
    tok = 16 * nb
    th = tok // 2
    right_steps, left_steps = NY // 2, (NY - 1) // 2

    v = lax.axis_index("vocab")
    w = lax.axis_index("width")
    c = lax.rem(v, NC)
    zh = lax.rem(lax.div(v, NC), NZH)
    y = lax.div(v, NC * NZH)
    x = lax.rem(w, NX)
    zl = lax.div(w, NX)
    yz = y * NZH + zh

    def dev(dy=0, dzh=0, dc=0, dzl=0, dx=0):
        yy = lax.rem(y + dy, NY)
        zz = lax.rem(zh + dzh, NZH)
        cc_ = lax.rem(c + dc, NC)
        ll = lax.rem(zl + dzl, NZL)
        xx = lax.rem(x + dx, NX)
        return ((yy * NZH + zz) * NC + cc_, ll * NX + xx)

    peers = []
    for dl in range(NZL):
        for dx in range(NX):
            for dc in range(NC):
                if dl or dx or dc:
                    peers.append(dict(dzl=dl, dx=dx, dc=dc))
    for d in range(1, NY):
        peers.append(dict(dy=d))
    for d in range(1, NZH):
        peers.append(dict(dzh=d))

    sends = []

    def push(src, dst, ssem, rsem, **where):
        d = pltpu.make_async_remote_copy(
            src_ref=src, dst_ref=dst, send_sem=ssem, recv_sem=rsem,
            device_id=dev(**where), device_id_type=MESH,
        )
        d.start()
        sends.append(d)

    def got(dst, rsem):
        pltpu.make_async_copy(dst, dst, rsem).wait()

    barrier = pltpu.get_barrier_semaphore()
    for p in peers:
        pl.semaphore_signal(barrier, inc=1, device_id=dev(**p), device_id_type=MESH)
    pl.semaphore_wait(barrier, len(peers))

    push(hid.at[:, pl.ds(pl.multiple_of((1 - c) * hf, 128), hf)], hsib, sib_s, sib_r, dc=1)
    locals_ = []

    def bring(src, dst, sem):
        d = pltpu.make_async_copy(src, dst, sem)
        d.start()
        locals_.append(d)
        return d

    mine_copy = pltpu.make_async_copy(
        hid.at[:, pl.ds(pl.multiple_of(c * hf, 128), hf)], hblk.at[0], loc.at[0]
    )
    mine_copy.start()
    mine_copy.wait()
    got(hsib, sib_r)
    mine = hblk[0].astype(f32)
    other = hsib[...].astype(f32)
    first = c == 0
    lo = jnp.where(first, mine, other)
    hi = jnp.where(first, other, mine)
    hown[0, :, 0:hf] = jnp.concatenate([lo, hi], axis=0).astype(bf16)
    block = hown.at[0, :, pl.ds(0, hf)]

    def spot(xx):
        return hg.at[yz, :, pl.ds(pl.multiple_of(c * hl + xx * hf, 128), hf)]

    for dx in range(1, NX):
        push(block, spot(x), hx_s.at[dx], hx_r.at[dx], dx=dx)
    spot_copy = pltpu.make_async_copy(block, spot(x), loc.at[1])
    spot_copy.start()

    arrays = (head, dirn)
    order = [(1, 0), (0, 0), (1, 1), (0, 1)]
    own_w = {}
    for arr, cc in order:
        for dx in range(1, NX):
            xx = lax.rem(x + dx, NX)
            push(
                arrays[arr].at[:, :, pl.ds(pl.multiple_of(xx * CW + cc * ch, 128), ch)],
                wb.at[arr, cc, :, x], w_s.at[arr, cc, dx], w_r.at[arr, cc, dx], dx=dx,
            )
        own_w[arr, cc] = pltpu.make_async_copy(
            arrays[arr].at[:, :, pl.ds(pl.multiple_of(x * CW + cc * ch, 128), ch)],
            wb.at[arr, cc, :, x], loc.at[2 + arr * 2 + cc],
        )
        own_w[arr, cc].start()
    keeps = []
    for xb in range(NX):
        for k, (src, dst) in enumerate(((dirn, dv), (res, rv))):
            d = pltpu.make_async_copy(
                src.at[:, :, pl.ds(xb * CW, CW)], dst.at[xb], loc.at[6 + 2 * xb + k]
            )
            d.start()
            keeps.append(d)

    spot_copy.wait()
    for dx in range(1, NX):
        got(spot(lax.rem(x + NX - dx, NX)), hx_r.at[dx])

    def slot(yy, zz, cc_):
        return hg.at[yy * NZH + zz, :, pl.ds(pl.multiple_of(cc_ * hl, 128), hl)]

    mine_slot = slot(y, zh, c)
    for d in range(1, NZH):
        push(mine_slot, mine_slot, hz_s.at[d], hz_r.at[d], dzh=d)

    def relay(ref, k, j):
        push(ref, ref, sb_s.at[k, j], sb_r.at[k, j], dc=1)

    for j in range(NZH):
        zz = lax.rem(zh + NZH - j, NZH)
        ref = slot(y, zz, c)
        if j:
            got(ref, hz_r.at[j])
        if right_steps:
            push(ref, ref, yr_s.at[0, 0, j], yr_r.at[0, 0, j], dy=1)
        if left_steps:
            push(ref, ref, yr_s.at[1, 0, j], yr_r.at[1, 0, j], dy=NY - 1)
        relay(ref, 0, j)
    ring = [(0, 0)]
    for s in range(1, right_steps + 1):
        for j in range(NZH):
            zz = lax.rem(zh + NZH - j, NZH)
            ref = slot(lax.rem(y + NY - s, NY), zz, c)
            got(ref, yr_r.at[0, s - 1, j])
            if s < right_steps:
                push(ref, ref, yr_s.at[0, s, j], yr_r.at[0, s, j], dy=1)
            relay(ref, s, j)
            if s <= left_steps:
                ref = slot(lax.rem(y + s, NY), zz, c)
                got(ref, yr_r.at[1, s - 1, j])
                if s < left_steps:
                    push(ref, ref, yr_s.at[1, s, j], yr_r.at[1, s, j], dy=NY - 1)
                relay(ref, right_steps + s, j)
    for j in range(NZH):
        zz = lax.rem(zh + NZH - j, NZH)
        for s in range(right_steps + 1):
            got(slot(lax.rem(y + NY - s, NY), zz, 1 - c), sb_r.at[s, j])
        for s in range(1, left_steps + 1):
            got(slot(lax.rem(y + s, NY), zz, 1 - c), sb_r.at[right_steps + s, j])

    for arr, cc in order:
        for dx in range(1, NX):
            got(wb.at[arr, cc, :, lax.rem(x + NX - dx, NX)], w_r.at[arr, cc, dx])
        own_w[arr, cc].wait()
        wm = wb[arr, cc].reshape(2 * hl, ch)
        hp = hg[pl.ds((1 - zl) * nb2, nb2)].reshape(th, 2 * hl)
        zs[arr, cc] = jnp.dot(hp, wm, preferred_element_type=f32)
        push(zs.at[arr, cc], zr.at[arr, cc], z_s.at[arr, cc], z_r.at[arr, cc], dzl=1)
        ho = hg[pl.ds(zl * nb2, nb2)].reshape(th, 2 * hl)
        own[arr, cc] = jnp.dot(ho, wm, preferred_element_type=f32)

    tails = []
    for h in range(2):
        d = pltpu.make_async_copy(
            hg.at[:, :, pl.ds(pl.multiple_of(h * hl + x * hf, 128), hf)],
            hown.at[:, :, pl.ds(h * hf, hf)], loc.at[6 + 2 * NX + h],
        )
        tails.append(d)
    for dx in range(1, NX):
        sends[dx].wait_send()
    for d in tails:
        d.start()

    for arr, cc in order:
        got(zr.at[arr, cc], z_r.at[arr, cc])
    for cc in range(2):
        for arr in range(2):
            own[arr, cc] = own[arr, cc] + zr[arr, cc]
    top = jnp.maximum(
        jnp.max(own[0, 0], axis=1, keepdims=True), jnp.max(own[0, 1], axis=1, keepdims=True)
    )
    total = jnp.zeros((th, 1), f32)
    moment = jnp.zeros((th, 1), f32)
    for cc in range(2):
        e = jnp.exp(own[0, cc] - top)
        own[0, cc] = e
        total = total + jnp.sum(e, axis=1, keepdims=True)
        moment = moment + jnp.sum(e * own[1, cc], axis=1, keepdims=True)
    lane = lax.broadcasted_iota(jnp.int32, (th, 128), 1)
    packed = jnp.where(lane == 0, top, jnp.where(lane == 1, total, moment))
    a1[0] = jnp.transpose(packed)[0:4]

    def merge(ref, n):
        tops = [ref[k, 0:1, :] for k in range(n)]
        m = tops[0]
        for t in tops[1:]:
            m = jnp.maximum(m, t)
        s = jnp.zeros_like(m)
        q = jnp.zeros_like(m)
        for k in range(n):
            g = jnp.exp(tops[k] - m)
            s = s + g * ref[k, 1:2, :]
            q = q + g * ref[k, 2:3, :]
        return m, s, q

    def put(ref, rows):
        for i, r in enumerate(rows):
            ref[0, i:i + 1, :] = r

    stage1 = [(dx, dc) for dx in range(NX) for dc in range(NC) if dx or dc]
    for dx, dc in stage1:
        k = dx * NC + dc
        push(a1.at[0], a1.at[k], a1_s.at[k], a1_r.at[k], dx=dx, dc=dc)
    for d in tails:
        d.wait()
    ht[...] = jnp.transpose(hown[...].reshape(tok, F).astype(f32)).astype(bf16)
    for dx, dc in stage1:
        k = dx * NC + dc
        got(a1.at[k], a1_r.at[k])
    put(a2, merge(a1, NX * NC))
    for d in range(1, NY):
        push(a2.at[0], a2.at[d], a2_s.at[d], a2_r.at[d], dy=d)
    for d in range(1, NY):
        got(a2.at[d], a2_r.at[d])
    put(a3, merge(a2, NY))
    for d in range(1, NZH):
        push(a3.at[0], a3.at[d], a3_s.at[d], a3_r.at[d], dzh=d)
    for d in range(1, NZH):
        got(a3.at[d], a3_r.at[d])
    m, s, q = merge(a3, NZH)
    folds = jnp.where(zl == 0, fold[:, 0:th], fold[:, th:2 * th])
    keep = (folds != 0).astype(f32)
    row = lax.broadcasted_iota(jnp.int32, (128, th), 0)
    back = jnp.transpose(jnp.where(row == 0, m, jnp.where(row == 1, keep / s, q / s)))
    factor = jnp.exp(top - back[:, 0:1]) * back[:, 1:2]
    mean = back[:, 2:3]
    for cc in range(2):
        cb[x, zl, :, cc * ch:(cc + 1) * ch] = (
            own[0, cc] * factor * (own[1, cc] - mean)
        ).astype(bf16)

    ol = 1 - zl
    xl, xr, xo = lax.rem(x + NX - 1, NX), lax.rem(x + 1, NX), lax.rem(x + 2, NX)

    def cpush(ref, i, **where):
        push(ref, ref, cx_s.at[i], cx_r.at[i], **where)

    me = cb.at[x, zl]
    push(me, me, cz_s, cz_r, dzl=1)
    if NX == 4:
        cpush(me, 0, dx=1)
        cpush(me, 1, dx=NX - 1)
    got(cb.at[x, ol], cz_r)
    if NX == 4:
        cpush(cb.at[x, ol], 2, dx=1)
        cpush(cb.at[x, ol], 3, dx=NX - 1)
        got(cb.at[xl, zl], cx_r.at[0])
        cpush(cb.at[xl, zl], 4, dx=1)

    for d in keeps:
        d.wait()

    sums = [jnp.zeros((1, CW), f32) for _ in range(4)]

    def image(xb, sums):
        block = jnp.dot(ht[...], cb[xb].reshape(tok, CW), preferred_element_type=f32)
        d = dv[xb].reshape(F, CW).astype(f32)
        r = rv[xb].reshape(F, CW).astype(f32)
        g = block + DAMPING * d
        img[xb] = g
        terms = (r * r, r * g, g * g, d * g)
        return [a + jnp.sum(t, axis=0, keepdims=True) for a, t in zip(sums, terms)]

    sums = image(x, sums)
    if NX == 4:
        got(cb.at[xr, ol], cx_r.at[3])
        cpush(cb.at[xr, ol], 5, dx=NX - 1)
        got(cb.at[xr, zl], cx_r.at[1])
        sums = image(xr, sums)
        got(cb.at[xl, ol], cx_r.at[2])
        sums = image(xl, sums)
        got(cb.at[xo, zl], cx_r.at[4])
        got(cb.at[xo, ol], cx_r.at[5])
        sums = image(xo, sums)

    put(b1, sums)
    stage1 = [
        (dl, dx, dc) for dl in range(NZL) for dx in range(NX) for dc in range(NC)
        if dl or dx or dc
    ]
    for dl, dx, dc in stage1:
        k = (dl * NX + dx) * NC + dc
        push(b1.at[0], b1.at[k], b1_s.at[k], b1_r.at[k], dx=dx, dc=dc, dzl=dl)
    for dl, dx, dc in stage1:
        k = (dl * NX + dx) * NC + dc
        got(b1.at[k], b1_r.at[k])

    def add(ref, n):
        s = ref[0]
        for k in range(1, n):
            s = s + ref[k]
        return s

    b2[0] = add(b1, NZL * NX * NC)
    for d in range(1, NY):
        push(b2.at[0], b2.at[d], b2_s.at[d], b2_r.at[d], dy=d)
    for d in range(1, NY):
        got(b2.at[d], b2_r.at[d])
    b3[0] = add(b2, NY)
    for d in range(1, NZH):
        push(b3.at[0], b3.at[d], b3_s.at[d], b3_r.at[d], dzh=d)
    for d in range(1, NZH):
        got(b3.at[d], b3_r.at[d])
    sums = jnp.sum(add(b3, NZH), axis=1, keepdims=True)
    rr, ri, ii, di = sums[0:1], sums[1:2], sums[2:3], sums[3:4]
    step = rr / di
    mixing = (rr + step * (step * ii - 2.0 * ri)) / rr
    for xb in range(NX):
        d = dv[xb].reshape(F, CW).astype(f32)
        r = rv[xb].reshape(F, CW).astype(f32)
        out[:, xb * CW:(xb + 1) * CW] = ((r - step * img[xb]) + mixing * d).astype(bf16)

    for i, d in enumerate(sends):
        if not 1 <= i < NX:
            d.wait_send()


def local(head_weight, direction, residual, hidden, fold_ids):
    f32, bf16 = jnp.float32, jnp.bfloat16
    hf, ch = F // 2, CW // 2
    nb = NY * NZH
    tok = 16 * nb
    th = tok // 2
    vd = NX * CW
    vm, dma = pltpu.VMEM, pltpu.SemaphoreType.DMA
    anyspace = pl.BlockSpec(memory_space=pl.ANY)
    vspace = pl.BlockSpec(memory_space=pltpu.VMEM)

    def pair(*shape):
        return [dma(shape) if shape else dma, dma(shape) if shape else dma]

    scratch = [
        vm((nb, 16, 2 * NX * hf), bf16),
        vm((2, 2, 2, NX, hf, ch), bf16),
        vm((NX, 2, hf, CW), bf16),
        vm((NX, 2, hf, CW), bf16),
        vm((NX, F, CW), f32),
        vm((NX, NZL, th, CW), bf16),
        vm((nb, 16, F), bf16),
        vm((F, tok), bf16),
        vm((8, hf), bf16),
        vm((1, 8, hf), bf16),
        vm((2, 2, th, ch), f32),
        vm((2, 2, th, ch), f32),
        vm((2, 2, th, ch), f32),
        vm((NX * NC, 4, th), f32),
        vm((NY, 4, th), f32),
        vm((NZH, 4, th), f32),
        vm((NZL * NX * NC, 4, CW), f32),
        vm((NY, 4, CW), f32),
        vm((NZH, 4, CW), f32),
        *pair(), *pair(NX), *pair(NZH), *pair(2, max(NY // 2, 1), NZH), *pair(NY, NZH),
        *pair(2, 2, NX), dma((8 + 2 * NX,)), *pair(2, 2), *pair(), *pair(6),
        *pair(NX * NC), *pair(NY), *pair(NZH),
        *pair(NZL * NX * NC), *pair(NY), *pair(NZH),
    ]
    return pl.pallas_call(
        kernel,
        out_shape=jax.ShapeDtypeStruct((F, vd), bf16),
        in_specs=[anyspace, anyspace, anyspace, vspace, vspace],
        out_specs=vspace,
        scratch_shapes=scratch,
        compiler_params=pltpu.CompilerParams(
            collective_id=0, has_side_effects=True, vmem_limit_bytes=48 * 1024 * 1024
        ),
    )(
        head_weight.reshape(2, hf, vd), direction.reshape(2, hf, vd),
        residual.reshape(2, hf, vd), hidden, fold_ids.reshape(1, tok),
    )


def solution(mesh):
    placed = (
        P("width", "vocab"),
        P("width", "vocab"),
        P("width", "vocab"),
        P("vocab", "width"),
        P(),
    )
    return jax.shard_map(
        local, mesh=mesh, in_specs=placed, out_specs=P("width", "vocab"), check_vma=False
    )
```

time: 571 us -> 104 us (0.18)
  blocking collectives: 436 us -> 0 us
  Pallas kernels: 0 us -> 97.9 us
  waiting for transfers between devices: 83.9 us -> 0 us
  between operations: 16.1 us -> 0.01 us
  matrix products: 10.4 us -> 0 us
  starting transfers between devices: 8.36 us -> 0 us
  other arithmetic: 7.74 us -> 0 us
    psum x3 -> x0, blocking collectives: 284 us -> none  [the longest x1 95.9 us: local(): lax.psum((jnp.sum(residual_wide * residual_wide), jnp.sum(direction_wide...]
    pallas_call x0 -> x1, Pallas kernels: none -> 97.9 us  [local(): pl.pallas_call(kernel, out_shape=jax.ShapeDtypeStruct((F, vd), bf16), in_...]
    pmax x1 -> x0, blocking collectives: 96.2 us -> none  [local(): row_top = lax.pmax(local_top, ('vocab', 'width'))]
    all_gather x1 -> x0, waiting for transfers between devices: 64 us -> none  [local(): panels = lax.all_gather(wide_panel, 'vocab', axis=0, tiled=True)]
    all_to_all x1 -> x0, blocking collectives: 29.6 us -> none  [local(): lax.all_to_all(column_block, 'width', split_axis=0, concat_axis=1, tiled=...]
    all_gather x1 -> x0, blocking collectives: 26.3 us -> none  [local(): wide_panel = lax.all_gather(hidden, 'width', axis=1, tiled=True)]
    all_to_all x2 -> x0, waiting for transfers between devices: 19.9 us -> none  [the longest x1 11.8 us: local(): lax.all_to_all(direction, 'width', split_axis=1, concat_axis=0, tiled=True)]
    dot_general x3 -> x0, matrix products: 10.4 us -> none  [the longest x1 3.72 us: local(): lax.dot_general(direction_cols, panels, CONTRACT_LEAD, preferred_element_...]
  transfers between devices with their start and end apart: 3 -> 0, of which waited for: 3 -> 0; matrix products, arithmetic and copies ran while one was open for 1% -> 0% of each run, Pallas kernels for 0% -> 0%
where the time goes in v1:
time: 104 us
  Pallas kernels  97.9 us (94%)
  local copies, waits for them, and re-layouts  6.02 us (6%)
    pallas_call x1, Pallas kernels, local(): pl.pallas_call(kernel, out_shape=jax.ShapeDtypeStruct((F, vd), bf16), in_...  97.9 us
    unnamed x11, local copies, waits for them, and re-layouts  6.02 us

profile of v1, /device:TPU:1, one launch (start us, length us, event | category | flops | bytes accessed | tf_op | source)
XLA Modules:
  0.0 104.0 jit_solution(12431271577112596597)
XLA Ops:
  0.0 0.0 copy-start.4
  0.0 0.7 copy-done.4
  0.7 0.0 copy-start
  0.7 1.2 %copy-done = bf16[512,1024]{1,0:T(8,128)(2,1)S(1)} copy-done((bf16[512,1024]{1,0:T(8,128)(2,1)S(1)}, bf16[512,1024]{1,0:T(8,128)(2,1)}, u32[]{:S(2)}) %copy-start) | copy-done | bytes 1048600
  1.9 0.0 copy-start.1
  1.9 1.2 %copy-done.1 = bf16[512,1024]{1,0:T(8,128)(2,1)S(1)} copy-done((bf16[512,1024]{1,0:T(8,128)(2,1)S(1)}, bf16[512,1024]{1,0:T(8,128)(2,1)}, u32[]{:S(2)}) %copy-start.1) | copy-done | bytes 1048600
  3.1 0.0 copy-start.2
  3.1 1.2 %copy-done.2 = bf16[512,1024]{1,0:T(8,128)(2,1)S(1)} copy-done((bf16[512,1024]{1,0:T(8,128)(2,1)S(1)}, bf16[512,1024]{1,0:T(8,128)(2,1)}, u32[]{:S(2)}) %copy-start.2) | copy-done | bytes 1048600
  4.4 0.0 copy-start.3
  4.4 0.7 copy-done.3
  5.1 97.9 %shard_map.55 = bf16[512,1024]{1,0:T(8,128)(2,1)S(1)} custom-call(bf16[2,256,1024]{2,1,0:T(8,128)(2,1)S(1)} %bitcast.4, bf16[2,256,1024]{2,1,0:T(8,128)(2,1)S(1)} %bitcast.5, bf16[2,256,1024]{2,1,0:T(8,128)(2,1)S(1)} %bitcast.6, bf16[8,512]{1,0:T(8,128)(2,1)S(1)} %copy-done.3, s32[1,512]{1,0:T(1,128)S(1)} %bitcast.7), custom_call_target="tpu_custom_call" | custom-call | tf_op jit(solution)/shard_map/pallas_call | solution.py:397
  103.0 1.0 copy.7
Async XLA Ops:
  0.0 0.7 copy-start.4
  0.7 1.2 %copy-start = (bf16[512,1024]{1,0:T(8,128)(2,1)S(1)}, bf16[512,1024]{1,0:T(8,128)(2,1)}, u32[]{:S(2)}) copy-start(bf16[512,1024]{1,0:T(8,128)(2,1)} %param.5) | copy-start | bytes 3145732
  1.9 1.2 %copy-start.1 = (bf16[512,1024]{1,0:T(8,128)(2,1)S(1)}, bf16[512,1024]{1,0:T(8,128)(2,1)}, u32[]{:S(2)}) copy-start(bf16[512,1024]{1,0:T(8,128)(2,1)} %param.6) | copy-start | bytes 3145732
  3.1 1.2 %copy-start.2 = (bf16[512,1024]{1,0:T(8,128)(2,1)S(1)}, bf16[512,1024]{1,0:T(8,128)(2,1)}, u32[]{:S(2)}) copy-start(bf16[512,1024]{1,0:T(8,128)(2,1)} %param.7) | copy-start | bytes 3145732
  4.4 0.7 copy-start.3

commit v2 on v0

v2 whole, which is shorter than its diff:
```python
import jax
import jax.numpy as jnp
from jax import lax
from jax.experimental import pallas as pl
from jax.experimental.pallas import tpu as pltpu
from jax.sharding import PartitionSpec as P

DAMPING = 0.02
MESH = pl.DeviceIdType.MESH
NY, NZH, NC, NZL, NX = 8, 4, 2, 2, 4
F = 512
CW = 256


def kernel(
    head, dirn, res, hid, fold_hbm, img_out, scal,
    fold, hp, hz, hq, hg, wb, dv, rv, img, cb, hown, ht, own, zs, zr, us, ur,
    a1, a2, a3, b1, b2, b3,
    hx_s, hx_r, hz_s, hz_r, yr_s, yr_r, sb_s, sb_r,
    w_s, w_r, loc, z_s, z_r, u_s, u_r, cz_s, cz_r, cx_s, cx_r,
    a1_s, a1_r, a2_s, a2_r, a3_s, a3_r,
    b1_s, b1_r, b2_s, b2_r, b3_s, b3_r,
):
    f32, bf16 = jnp.float32, jnp.bfloat16
    hf = F // 2
    hl = NX * hf
    nb = NY * NZH
    nb2 = nb // 2
    tok = 16 * nb
    th = tok // 2
    qt = th // 2
    nz = NZH * NZL

    v = lax.axis_index("vocab")
    w = lax.axis_index("width")
    c = lax.rem(v, NC)
    zh = lax.rem(lax.div(v, NC), NZH)
    y = lax.div(v, NC * NZH)
    x = lax.rem(w, NX)
    zl = lax.div(w, NX)
    z = zh * NZL + zl

    xs = [x] + [lax.rem(x + d, NX) for d in range(1, NX)]
    ys = [y] + [lax.rem(y + d, NY) for d in range(1, NY)]
    hs = [zh] + [lax.rem(zh + d, NZH) for d in range(1, NZH)]
    cs = [c, 1 - c]
    ls = [zl, 1 - zl]
    zs_ = [z] + [lax.rem(z + d, nz) for d in range(1, nz)]
    vy = [i * (NZH * NC) for i in ys]
    vh = [i * NC for i in hs]
    wl = [i * NX for i in ls]

    def dev(dy=0, dzh=0, dc=0, dzl=0, dx=0, dz=0):
        if dz:
            hh = lax.div(zs_[dz], NZL)
            return (vy[dy] + hh * NC + cs[dc], (zs_[dz] - hh * NZL) * NX + xs[dx])
        return (vy[dy] + vh[dzh] + cs[dc], wl[dzl] + xs[dx])

    near = [(dx, dc) for dx in range(NX) for dc in range(NC) if dx or dc]
    peers = [dict(dx=dx, dc=dc) for dx, dc in near]
    peers += [dict(dy=d) for d in sorted({1, NY - 1})]
    peers += [dict(dzh=d) for d in range(1, NZH)]
    peers += [dict(dzl=1)]

    sends = []

    def push(src, dst, ssem, rsem, **where):
        d = pltpu.make_async_remote_copy(
            src_ref=src, dst_ref=dst, send_sem=ssem, recv_sem=rsem,
            device_id=dev(**where), device_id_type=MESH,
        )
        d.start()
        sends.append(d)

    def got(dst, rsem):
        pltpu.make_async_copy(dst, dst, rsem).wait()

    def bring(src, dst, i):
        d = pltpu.make_async_copy(src, dst, loc.at[i])
        d.start()
        return d

    barrier = pltpu.get_barrier_semaphore()
    for p in peers:
        pl.semaphore_signal(barrier, inc=1, device_id=dev(**p), device_id_type=MESH)
    own_piece = bring(hid.at[:, pl.ds(pl.multiple_of(c * hf, 128), hf)], hp.at[x, c, 0], 0)
    keeps = [bring(fold_hbm, fold, 1)]
    for xb in range(NX):
        keeps.append(bring(dirn.at[:, :, pl.ds(xb * CW, CW)], dv.at[xb], 2 + 2 * xb))
        keeps.append(bring(res.at[:, :, pl.ds(xb * CW, CW)], rv.at[xb], 3 + 2 * xb))
    own_w = {}
    arrays = (head, dirn)
    for arr in (1, 0):
        own_w[arr] = bring(
            arrays[arr].at[:, :, pl.ds(pl.multiple_of(x * CW, 128), CW)],
            wb.at[arr, :, x], 2 + 2 * NX + arr,
        )
    pl.semaphore_wait(barrier, len(peers))

    parts = [pl.multiple_of(i * hf, 128) for i in cs]
    for dx, dc in near:
        k = dx * NC + dc
        push(
            hid.at[:, pl.ds(parts[dc], hf)], hp.at[x, c, 0],
            hx_s.at[0, k], hx_r.at[0, k], dx=dx, dc=dc,
        )
    for d in range(1, NZH):
        push(hid, hz.at[d], hz_s.at[d], hz_r.at[d], dzh=d)

    def columns(arr, h):
        for dx in (1, 3, 2)[:NX - 1]:
            cols = pl.ds(pl.multiple_of(xs[dx] * CW, 128), CW)
            push(
                arrays[arr].at[h, :, cols], wb.at[arr, h, x],
                w_s.at[arr, h, dx], w_r.at[arr, h, dx], dx=dx,
            )

    columns(1, 0)
    own_piece.wait()

    def slot(yy, zz, cc):
        return hg.at[yy * NZH + zz, :, pl.ds(pl.multiple_of(cc * hl, 128), hl)]

    def at(k, j, cc):
        return slot(ys[-k % NY], hs[-j % NZH], cc)

    def collect(first, n):
        for dx, dc in near:
            got(
                hp.at[xs[-dx % NX], cs[dc], pl.ds(first, n)],
                hx_r.at[min(first, 1), dx * NC + dc],
            )
        for j in range(first, first + n):
            for xb in range(NX):
                hq[j, :, xb * hf:(xb + 1) * hf] = jnp.concatenate(
                    [hp[xb, 0, j].astype(f32), hp[xb, 1, j].astype(f32)], axis=0
                ).astype(bf16)
            keeps.append(bring(hq.at[j], at(0, j, c), 7 + 3 * NX + j))

    last = {(0, j): NY // 2 - (0 if 2 * j <= NZH - 1 else 1) for j in range(NZH)}
    last.update({(1, j): NY - 1 - last[0, j] for j in range(NZH)})
    free = [0.0, 0.0]
    events = []

    def ring(src, k, j, way, s, now):
        if s < last[way, j]:
            dst = at(k, j, c)
            push(src, dst, yr_s.at[way, s, j], yr_r.at[way, s, j], dy=(1, NY - 1)[way])
            begin = max(now, free[way])
            free[way] = begin + 0.8
            events.append((begin + 2.4, len(events), way, s + 1, j))

    def arrive(src, k, j, ways, s, now):
        for way in ways:
            ring(src, k, j, way, s, now)
        push(src, at(k, j, c), sb_s.at[k, j], sb_r.at[k, j], dc=1)

    collect(0, 1)
    arrive(hq.at[0], 0, 0, (0, 1), 0, 0.0)
    for d in range(1, NZH):
        got(hz.at[d], hz_r.at[d])
    if NZH > 1:
        rest = pl.ds(1, NZH - 1)
        for dx, dc in near:
            k = dx * NC + dc
            push(
                hz.at[rest, :, pl.ds(parts[dc], hf)], hp.at[x, c, rest],
                hx_s.at[1, k], hx_r.at[1, k], dx=dx, dc=dc,
            )
        rest_copy = bring(hz.at[rest, :, pl.ds(parts[0], hf)], hp.at[x, c, rest], 4 + 2 * NX)
        events.append((4.5, len(events), 2, 0, 1))
    columns(1, 1)
    columns(0, 0)
    columns(0, 1)
    done = set()
    while len(done) < len(events):
        now, tag, way, s, j = min(e for e in events if e[1] not in done)
        done.add(tag)
        if way == 2:
            rest_copy.wait()
            collect(1, NZH - 1)
            for j in range(1, NZH):
                arrive(hq.at[j], 0, j, (0, 1), 0, now)
        else:
            k = s if way == 0 else NY - s
            got(at(k, j, c), yr_r.at[way, s - 1, j])
            arrive(at(k, j, c), k, j, (way,), s, now)
    for k in range(NY):
        for j in range(NZH):
            got(at(k, j, 1 - c), sb_r.at[k, j])
    for d in keeps:
        d.wait()

    for arr in (1, 0):
        for h in range(2):
            for dx in range(1, NX):
                got(wb.at[arr, h, xs[-dx % NX]], w_r.at[arr, h, dx])
        own_w[arr].wait()
        for h in range(2):
            rows = hg[pl.ds((1 - zl) * nb2 + h * (nb2 // 2), nb2 // 2)].reshape(qt, 2 * hl)
            part = jnp.dot(rows, wb[arr].reshape(2 * hl, CW), preferred_element_type=f32)
            reach = jnp.maximum(jnp.max(jnp.abs(part), axis=1, keepdims=True), 1e-30)
            steps = (part * (32767.0 / reach) + 32768.5).astype(jnp.int32) - 32768
            zs[arr, h] = steps.astype(jnp.int16)
            push(zs.at[arr, h], zr.at[arr, h], z_s.at[arr, h], z_r.at[arr, h], dzl=1)
            wide = jnp.broadcast_to(reach * (1.0 / 32767.0), (qt, 128))
            us[arr, h] = jnp.transpose(wide)[0:1]
            push(us.at[arr, h], ur.at[arr, h], u_s.at[arr, h], u_r.at[arr, h], dzl=1)
        rows = hg[pl.ds(zl * nb2, nb2)].reshape(th, 2 * hl)
        own[arr] = jnp.dot(rows, wb[arr].reshape(2 * hl, CW), preferred_element_type=f32)

    tails = [
        bring(
            hg.at[:, :, pl.ds(pl.multiple_of(h * hl + x * hf, 128), hf)],
            hown.at[:, :, pl.ds(h * hf, hf)], 5 + 2 * NX + h,
        )
        for h in range(2)
    ]
    for d in tails:
        d.wait()
    ht[...] = jnp.transpose(hown[...].reshape(tok, F).astype(f32)).astype(bf16)

    def whole(arr):
        parts = []
        for h in range(2):
            got(ur.at[arr, h], u_r.at[arr, h])
            unit = jnp.transpose(jnp.broadcast_to(ur[arr, h], (128, qt)))[:, 0:1]
            got(zr.at[arr, h], z_r.at[arr, h])
            parts.append(
                own[arr, h * qt:(h + 1) * qt] + zr[arr, h].astype(jnp.int32).astype(f32) * unit
            )
        return jnp.concatenate(parts, axis=0)

    tangent = whole(1)
    logits = whole(0)
    top = jnp.max(logits, axis=1, keepdims=True)
    e = jnp.exp(logits - top)
    total = jnp.sum(e, axis=1, keepdims=True)
    moment = jnp.sum(e * tangent, axis=1, keepdims=True)
    own[0] = e
    own[1] = tangent
    lane = lax.broadcasted_iota(jnp.int32, (th, 128), 1)
    packed = jnp.where(lane == 0, top, jnp.where(lane == 1, total, moment))
    a1[0] = jnp.transpose(packed)[0:4]

    def merge(ref, n):
        tops = [ref[k, 0:1, :] for k in range(n)]
        m = tops[0]
        for t in tops[1:]:
            m = jnp.maximum(m, t)
        s = jnp.zeros_like(m)
        q = jnp.zeros_like(m)
        for k in range(n):
            g = jnp.exp(tops[k] - m)
            s = s + g * ref[k, 1:2, :]
            q = q + g * ref[k, 2:3, :]
        return m, s, q

    def put(ref, rows):
        for i, r in enumerate(rows):
            ref[0, i:i + 1, :] = r

    def share(ref, ssems, rsems, moves):
        for k, where in moves:
            push(ref.at[0], ref.at[k], ssems.at[k], rsems.at[k], **where)
        for k, where in moves:
            got(ref.at[k], rsems.at[k])

    over_x = [(dx * NC + dc, dict(dx=dx, dc=dc)) for dx, dc in near]
    over_y = [(d, dict(dy=d)) for d in range(1, NY)]
    over_zh = [(d, dict(dzh=d)) for d in range(1, NZH)]
    over_z = [(d, dict(dz=d)) for d in range(1, nz)]
    share(a1, a1_s, a1_r, over_x)
    put(a2, merge(a1, NX * NC))
    share(a2, a2_s, a2_r, over_y)
    put(a3, merge(a2, NY))
    share(a3, a3_s, a3_r, over_zh)
    m, s, q = merge(a3, NZH)
    folds = jnp.where(zl == 0, fold[:, 0:th], fold[:, th:2 * th])
    keep = (folds != 0).astype(f32)
    row = lax.broadcasted_iota(jnp.int32, (128, th), 0)
    back = jnp.transpose(jnp.where(row == 0, m, jnp.where(row == 1, keep / s, q / s)))
    factor = jnp.exp(top - back[:, 0:1]) * back[:, 1:2]
    curving = (own[0] * factor * (own[1] - back[:, 2:3])).astype(bf16)
    cb[x, zl] = curving.reshape(2, qt, CW)

    ol = ls[1]
    xl, xr, xo = xs[-1], xs[1 % NX], xs[2 % NX]
    ahead, behind = dict(dx=1), dict(dx=NX - 1)

    def cpush(xx, ll, h, i, where):
        ref = cb.at[xx, ll, h]
        push(ref, ref, cx_s.at[i], cx_r.at[i], **where)

    def cgot(xx, ll, h, i):
        got(cb.at[xx, ll, h], cx_r.at[i])

    for h in range(2):
        me = cb.at[x, zl, h]
        push(me, me, cz_s.at[h], cz_r.at[h], dzl=1)
        if NX == 4:
            cpush(x, zl, h, h, ahead)
            cpush(x, zl, h, 2 + h, behind)
    got(cb.at[x, ol, 0], cz_r.at[0])
    if NX == 4:
        cpush(x, ol, 0, 4, ahead)
        cpush(x, ol, 0, 6, behind)
        cgot(xl, zl, 0, 0)
        cpush(xl, zl, 0, 8, ahead)
    got(cb.at[x, ol, 1], cz_r.at[1])
    if NX == 4:
        cpush(x, ol, 1, 7, behind)
        cgot(xr, zl, 1, 3)
        cpush(xr, zl, 1, 9, behind)
        cpush(x, ol, 1, 5, ahead)

    sums = [jnp.zeros((1, 128), f32) for _ in range(4)]
    img_moves = []

    def image(xb, sums):
        block = jnp.dot(ht[...], cb[xb].reshape(tok, CW), preferred_element_type=f32)
        d = dv[xb].reshape(F, CW).astype(f32)
        r = rv[xb].reshape(F, CW).astype(f32)
        g = block + DAMPING * d
        img[xb] = g
        img_moves.append(
            bring(
                img.at[xb], img_out.at[:, pl.ds(pl.multiple_of(xb * CW, 128), CW)],
                7 + 2 * NX + len(img_moves),
            )
        )
        terms = (r * r, r * g, g * g, d * g)
        rows = [jnp.sum(t, axis=0, keepdims=True) for t in terms]
        for i in range(0, CW, 128):
            sums = [a + t[:, i:i + 128] for a, t in zip(sums, rows)]
        return sums

    sums = image(x, sums)
    if NX == 4:
        cgot(xl, ol, 0, 4)
        cpush(xl, ol, 0, 10, ahead)
        cgot(xr, ol, 1, 7)
        cpush(xr, ol, 1, 11, behind)
        cgot(xl, zl, 1, 1)
        cgot(xl, ol, 1, 5)
        sums = image(xl, sums)
        cgot(xr, zl, 0, 2)
        cgot(xr, ol, 0, 6)
        sums = image(xr, sums)
        cgot(xo, zl, 0, 8)
        cgot(xo, zl, 1, 9)
        cgot(xo, ol, 0, 10)
        cgot(xo, ol, 1, 11)
        sums = image(xo, sums)

    def add(ref, n):
        s = ref[0]
        for k in range(1, n):
            s = s + ref[k]
        return s

    put(b1, sums)
    share(b1, b1_s, b1_r, over_x)
    b2[0] = add(b1, NX * NC)
    share(b2, b2_s, b2_r, over_y)
    b3[0] = add(b2, NY)
    share(b3, b3_s, b3_r, over_z)
    sums = jnp.sum(add(b3, nz), axis=1, keepdims=True)
    rr, ri, ii, di = sums[0:1], sums[1:2], sums[2:3], sums[3:4]
    step = rr / di
    mixing = (rr + step * (step * ii - 2.0 * ri)) / rr
    scal[0:1, :] = jnp.broadcast_to(step, (1, 128))
    scal[1:2, :] = jnp.broadcast_to(mixing, (1, 128))

    for d in img_moves:
        d.wait()
    for d in sends:
        d.wait_send()


def local(head_weight, direction, residual, hidden, fold_ids):
    f32, bf16 = jnp.float32, jnp.bfloat16
    hf = F // 2
    nb = NY * NZH
    tok = 16 * nb
    th = tok // 2
    vd = NX * CW
    vm, dma = pltpu.VMEM, pltpu.SemaphoreType.DMA
    anyspace = pl.BlockSpec(memory_space=pltpu.HBM)
    vspace = pl.BlockSpec(memory_space=pltpu.VMEM)

    def pair(*shape):
        return [dma(shape) if shape else dma, dma(shape) if shape else dma]

    scratch = [
        vm((1, tok), jnp.int32),
        vm((NX, NC, NZH, 8, hf), bf16),
        vm((NZH, 8, F), bf16),
        vm((NZH, 16, NX * hf), bf16),
        vm((nb, 16, 2 * NX * hf), bf16),
        vm((2, 2, NX, hf, CW), bf16),
        vm((NX, 2, hf, CW), bf16),
        vm((NX, 2, hf, CW), bf16),
        vm((NX, F, CW), f32),
        vm((NX, NZL, 2, th // 2, CW), bf16),
        vm((nb, 16, F), bf16),
        vm((F, tok), bf16),
        vm((2, th, CW), f32),
        vm((2, 2, th // 2, CW), jnp.int16),
        vm((2, 2, th // 2, CW), jnp.int16),
        vm((2, 2, 1, th // 2), f32),
        vm((2, 2, 1, th // 2), f32),
        vm((NX * NC, 4, th), f32),
        vm((NY, 4, th), f32),
        vm((NZH, 4, th), f32),
        vm((NX * NC, 4, 128), f32),
        vm((NY, 4, 128), f32),
        vm((NZH * NZL, 4, 128), f32),
        *pair(2, NX * NC), *pair(NZH), *pair(2, max(NY // 2, 1), NZH), *pair(NY, NZH),
        *pair(2, 2, NX), dma((7 + 3 * NX + NZH,)), *pair(2, 2), *pair(2, 2), *pair(2), *pair(12),
        *pair(NX * NC), *pair(NY), *pair(NZH),
        *pair(NX * NC), *pair(NY), *pair(NZH * NZL),
    ]
    image, scalars = pl.pallas_call(
        kernel,
        out_shape=(
            jax.ShapeDtypeStruct((F, vd), f32), jax.ShapeDtypeStruct((2, 128), f32)
        ),
        in_specs=[anyspace] * 5,
        out_specs=(anyspace, vspace),
        scratch_shapes=scratch,
        compiler_params=pltpu.CompilerParams(
            collective_id=0, has_side_effects=True, vmem_limit_bytes=67043328
        ),
    )(
        head_weight.reshape(2, hf, vd), direction.reshape(2, hf, vd),
        residual.reshape(2, hf, vd), hidden, fold_ids.reshape(1, tok),
    )
    moved = residual.astype(f32) - scalars[0:1, 0:1] * image
    return (moved + scalars[1:2, 0:1] * direction.astype(f32)).astype(bf16)


def solution(mesh):
    placed = (
        P("width", "vocab"),
        P("width", "vocab"),
        P("width", "vocab"),
        P("vocab", "width"),
        P(),
    )
    return jax.shard_map(
        local, mesh=mesh, in_specs=placed, out_specs=P("width", "vocab"), check_vma=False
    )
```

time: 571 us -> 95.9 us (0.17)
  blocking collectives: 436 us -> 0 us
  Pallas kernels: 0 us -> 89.3 us
  waiting for transfers between devices: 83.9 us -> 0 us
  between operations: 16.1 us -> 0.01 us
  matrix products: 10.4 us -> 0 us
  starting transfers between devices: 8.36 us -> 0 us
  local copies, waits for them, and re-layouts: 8.15 us -> 1.33 us
    psum x3 -> x0, blocking collectives: 284 us -> none  [the longest x1 95.9 us: local(): lax.psum((jnp.sum(residual_wide * residual_wide), jnp.sum(direction_wide...]
    pmax x1 -> x0, blocking collectives: 96.2 us -> none  [local(): row_top = lax.pmax(local_top, ('vocab', 'width'))]
    pallas_call x0 -> x1, Pallas kernels: none -> 89.3 us  [local(): pl.pallas_call(kernel, out_shape=(jax.ShapeDtypeStruct((F, vd), f32), jax...]
    all_gather x1 -> x0, waiting for transfers between devices: 64 us -> none  [local(): panels = lax.all_gather(wide_panel, 'vocab', axis=0, tiled=True)]
    all_to_all x1 -> x0, blocking collectives: 29.6 us -> none  [local(): lax.all_to_all(column_block, 'width', split_axis=0, concat_axis=1, tiled=...]
    all_gather x1 -> x0, blocking collectives: 26.3 us -> none  [local(): wide_panel = lax.all_gather(hidden, 'width', axis=1, tiled=True)]
    all_to_all x2 -> x0, waiting for transfers between devices: 19.9 us -> none  [the longest x1 11.8 us: local(): lax.all_to_all(direction, 'width', split_axis=1, concat_axis=0, tiled=True)]
    dot_general x3 -> x0, matrix products: 10.4 us -> none  [the longest x1 3.72 us: local(): lax.dot_general(direction_cols, panels, CONTRACT_LEAD, preferred_element_...]
  transfers between devices with their start and end apart: 3 -> 0, of which waited for: 3 -> 0; matrix products, arithmetic and copies ran while one was open for 1% -> 0% of each run, Pallas kernels for 0% -> 0%
where the time goes in v2:
time: 95.9 us; the launch traced here: 95.5 us
  Pallas kernels  89.3 us (93%)
  other arithmetic  4.85 us (5%)
  local copies, waits for them, and re-layouts  1.33 us (1%)
    pallas_call x1, Pallas kernels, local(): pl.pallas_call(kernel, out_shape=(jax.ShapeDtypeStruct((F, vd), f32), jax...  89.3 us
    convert_element_type x1, other arithmetic, local(): return (moved + scalars[1:2, 0:1] * direction.astype(f32)).astype(bf16)  4.85 us

profile of v2, /device:TPU:1, one launch (start us, length us, event | category | flops | bytes accessed | tf_op | source)
XLA Modules:
  0.0 95.5 jit_solution(3206253764107561174)
XLA Ops:
  0.0 89.3 %shard_map.55 = (f32[512,1024]{1,0:T(8,128)}, f32[2,128]{1,0:T(2,128)}) custom-call(bf16[2,256,1024]{2,1,0:T(8,128)(2,1)} %bitcast.8, bf16[2,256,1024]{2,1,0:T(8,128)(2,1)} %bitcast.6, bf16[2,256,1024]{2,1,0:T(8,128)(2,1)} %bitcast.7, bf16[8,512]{1,0:T(8,128)(2,1)} %hid.1, s32[1,512]{1,0:T(1,128)} %bitcast.9), custom_call_target="tpu_custom_call" | custom-call | tf_op jit(solution)/shard_map/pallas_call | solution.py:424
  89.3 1.3 %fusion = (f32[1,1]{1,0:T(1,128)}, f32[1,1]{1,0:T(1,128)}) fusion(f32[2,128]{1,0:T(2,128)} %get-tuple-element.7), kind=kLoop, calls=%fused_computation.1 | loop fusion | bytes 16 | tf_op jit(solution)/shard_map/slice | solution.py:439
  90.7 4.9 %add_convert_fusion = bf16[512,1024]{1,0:T(8,128)(2,1)} fusion(bf16[512,1024]{1,0:T(8,128)(2,1)} %param.6, f32[512,1024]{1,0:T(8,128)} %get-tuple-element.8, bf16[512,1024]{1,0:T(8,128)(2,1)} %param.7, f32[]{:T(128)} %bitcast.5, f32[]{:T(128)} %bitcast.4), kind=kLoop, calls=%fused_computation | loop fusion | flops 3670016 | bytes 5242888 | tf_op jit(solution)/shard_map/convert_element_type | solution.py:440

commit v3 on v2

--- a/solution.py
+++ b/solution.py
@@ -13,7 +13,7 @@
 
 
 def kernel(
-    head, dirn, res, hid, fold_hbm, img_out, scal,
+    head, dirn, res, hid, fold_hbm, out,
     fold, hp, hz, hq, hg, wb, dv, rv, img, cb, hown, ht, own, zs, zr, us, ur,
     a1, a2, a3, b1, b2, b3,
     hx_s, hx_r, hz_s, hz_r, yr_s, yr_r, sb_s, sb_r,
@@ -83,7 +83,7 @@
     barrier = pltpu.get_barrier_semaphore()
     for p in peers:
         pl.semaphore_signal(barrier, inc=1, device_id=dev(**p), device_id_type=MESH)
-    own_piece = bring(hid.at[:, pl.ds(pl.multiple_of(c * hf, 128), hf)], hp.at[x, c, 0], 0)
+    own_hid = bring(hid, hz.at[0], 0)
     keeps = [bring(fold_hbm, fold, 1)]
     for xb in range(NX):
         keeps.append(bring(dirn.at[:, :, pl.ds(xb * CW, CW)], dv.at[xb], 2 + 2 * xb))
@@ -95,17 +95,18 @@
             arrays[arr].at[:, :, pl.ds(pl.multiple_of(x * CW, 128), CW)],
             wb.at[arr, :, x], 2 + 2 * NX + arr,
         )
+    own_hid.wait()
     pl.semaphore_wait(barrier, len(peers))
 
     parts = [pl.multiple_of(i * hf, 128) for i in cs]
     for dx, dc in near:
         k = dx * NC + dc
         push(
-            hid.at[:, pl.ds(parts[dc], hf)], hp.at[x, c, 0],
+            hz.at[0, :, pl.ds(parts[dc], hf)], hp.at[x, c, 0],
             hx_s.at[0, k], hx_r.at[0, k], dx=dx, dc=dc,
         )
     for d in range(1, NZH):
-        push(hid, hz.at[d], hz_s.at[d], hz_r.at[d], dzh=d)
+        push(hz.at[0], hz.at[d], hz_s.at[d], hz_r.at[d], dzh=d)
 
     def columns(arr, h):
         for dx in (1, 3, 2)[:NX - 1]:
@@ -116,6 +117,7 @@
             )
 
     columns(1, 0)
+    own_piece = bring(hz.at[0, :, pl.ds(parts[0], hf)], hp.at[x, c, 0], 0)
     own_piece.wait()
 
     def slot(yy, zz, cc):
@@ -206,6 +208,7 @@
             wide = jnp.broadcast_to(reach * (1.0 / 32767.0), (qt, 128))
             us[arr, h] = jnp.transpose(wide)[0:1]
             push(us.at[arr, h], ur.at[arr, h], u_s.at[arr, h], u_r.at[arr, h], dzl=1)
+    for arr in (1, 0):
         rows = hg[pl.ds(zl * nb2, nb2)].reshape(th, 2 * hl)
         own[arr] = jnp.dot(rows, wb[arr].reshape(2 * hl, CW), preferred_element_type=f32)
 
@@ -231,6 +234,12 @@
             )
         return jnp.concatenate(parts, axis=0)
 
+    squares = jnp.zeros((1, 128), f32)
+    for xb in range(NX):
+        r = rv[xb].reshape(F, CW).astype(f32)
+        t = jnp.sum(r * r, axis=0, keepdims=True)
+        for i in range(0, CW, 128):
+            squares = squares + t[:, i:i + 128]
     tangent = whole(1)
     logits = whole(0)
     top = jnp.max(logits, axis=1, keepdims=True)
@@ -314,8 +323,7 @@
         cpush(xr, zl, 1, 9, behind)
         cpush(x, ol, 1, 5, ahead)
 
-    sums = [jnp.zeros((1, 128), f32) for _ in range(4)]
-    img_moves = []
+    sums = [jnp.zeros((1, 128), f32) for _ in range(3)]
 
     def image(xb, sums):
         block = jnp.dot(ht[...], cb[xb].reshape(tok, CW), preferred_element_type=f32)
@@ -323,13 +331,7 @@
         r = rv[xb].reshape(F, CW).astype(f32)
         g = block + DAMPING * d
         img[xb] = g
-        img_moves.append(
-            bring(
-                img.at[xb], img_out.at[:, pl.ds(pl.multiple_of(xb * CW, 128), CW)],
-                7 + 2 * NX + len(img_moves),
-            )
-        )
-        terms = (r * r, r * g, g * g, d * g)
+        terms = (r * g, g * g, d * g)
         rows = [jnp.sum(t, axis=0, keepdims=True) for t in terms]
         for i in range(0, CW, 128):
             sums = [a + t[:, i:i + 128] for a, t in zip(sums, rows)]
@@ -359,7 +361,7 @@
             s = s + ref[k]
         return s
 
-    put(b1, sums)
+    put(b1, [squares] + sums)
     share(b1, b1_s, b1_r, over_x)
     b2[0] = add(b1, NX * NC)
     share(b2, b2_s, b2_r, over_y)
@@ -369,11 +371,11 @@
     rr, ri, ii, di = sums[0:1], sums[1:2], sums[2:3], sums[3:4]
     step = rr / di
     mixing = (rr + step * (step * ii - 2.0 * ri)) / rr
-    scal[0:1, :] = jnp.broadcast_to(step, (1, 128))
-    scal[1:2, :] = jnp.broadcast_to(mixing, (1, 128))
-
-    for d in img_moves:
-        d.wait()
+    for xb in range(NX):
+        d = dv[xb].reshape(F, CW).astype(f32)
+        r = rv[xb].reshape(F, CW).astype(f32)
+        out[:, xb * CW:(xb + 1) * CW] = ((r - step * img[xb]) + mixing * d).astype(bf16)
+
     for d in sends:
         d.wait_send()
 
@@ -421,13 +423,11 @@
         *pair(NX * NC), *pair(NY), *pair(NZH),
         *pair(NX * NC), *pair(NY), *pair(NZH * NZL),
     ]
-    image, scalars = pl.pallas_call(
+    return pl.pallas_call(
         kernel,
-        out_shape=(
-            jax.ShapeDtypeStruct((F, vd), f32), jax.ShapeDtypeStruct((2, 128), f32)
-        ),
+        out_shape=jax.ShapeDtypeStruct((F, vd), bf16),
         in_specs=[anyspace] * 5,
-        out_specs=(anyspace, vspace),
+        out_specs=vspace,
         scratch_shapes=scratch,
         compiler_params=pltpu.CompilerParams(
             collective_id=0, has_side_effects=True, vmem_limit_bytes=67043328
@@ -436,8 +436,6 @@
         head_weight.reshape(2, hf, vd), direction.reshape(2, hf, vd),
         residual.reshape(2, hf, vd), hidden, fold_ids.reshape(1, tok),
     )
-    moved = residual.astype(f32) - scalars[0:1, 0:1] * image
-    return (moved + scalars[1:2, 0:1] * direction.astype(f32)).astype(bf16)
 
 
 def solution(mesh):

time: 95.9 us -> 93 us (0.970)
  other arithmetic: 4.85 us -> 0 us
  Pallas kernels: 89.3 us -> 90.3 us
    convert_element_type x1 -> x0, other arithmetic: 4.85 us -> none  [local(): return (moved + scalars[1:2, 0:1] * direction.astype(f32)).astype(bf16)]
    unnamed x0 -> x1, local copies, waits for them, and re-layouts: none -> 2.26 us
    slice x1 -> x0, local copies, waits for them, and re-layouts: 1.33 us -> none  [local(): moved = residual.astype(f32) - scalars[0:1, 0:1] * image]
    pallas_call x1, Pallas kernels: 89.3 us -> 90.3 us  [local(): pl.pallas_call(kernel, out_shape=jax.ShapeDtypeStruct((F, vd), bf16), in_...]
where the time goes in v3:
time: 93 us; the launch traced here: 92.6 us
  Pallas kernels  90.3 us (97%)
  local copies, waits for them, and re-layouts  2.26 us (2%)
    pallas_call x1, Pallas kernels, local(): pl.pallas_call(kernel, out_shape=jax.ShapeDtypeStruct((F, vd), bf16), in_...  90.3 us
    unnamed x1, local copies, waits for them, and re-layouts  2.26 us

profile of v3, /device:TPU:1, one launch (start us, length us, event | category | flops | bytes accessed | tf_op | source)
XLA Modules:
  0.0 92.6 jit_solution(4174830655317280466)
XLA Ops:
  0.0 90.3 %shard_map.55 = bf16[512,1024]{1,0:T(8,128)(2,1)} custom-call(bf16[2,256,1024]{2,1,0:T(8,128)(2,1)} %bitcast.4, bf16[2,256,1024]{2,1,0:T(8,128)(2,1)} %bitcast.5, bf16[2,256,1024]{2,1,0:T(8,128)(2,1)} %bitcast.6, bf16[8,512]{1,0:T(8,128)(2,1)} %hid.1, s32[1,512]{1,0:T(1,128)} %bitcast.7), custom_call_target="tpu_custom_call" | custom-call | tf_op jit(solution)/shard_map/pallas_call | solution.py:426
  90.3 2.3 %copy.7 = bf16[512,1024]{1,0:T(8,128)(2,1)} copy(bf16[512,1024]{1,0:T(8,128)(2,1)} %shard_map.55) | data formatting | bytes 2097152

commit v4 on v3

--- a/solution.py
+++ b/solution.py
@@ -108,15 +108,15 @@
     for d in range(1, NZH):
         push(hz.at[0], hz.at[d], hz_s.at[d], hz_r.at[d], dzh=d)
 
-    def columns(arr, h):
-        for dx in (1, 3, 2)[:NX - 1]:
+    def columns(arr, h, ways=(1, 3, 2)):
+        for dx in ways[:NX - 1]:
             cols = pl.ds(pl.multiple_of(xs[dx] * CW, 128), CW)
             push(
                 arrays[arr].at[h, :, cols], wb.at[arr, h, x],
                 w_s.at[arr, h, dx], w_r.at[arr, h, dx], dx=dx,
             )
 
-    columns(1, 0)
+    columns(1, 0, (1, 3))
     own_piece = bring(hz.at[0, :, pl.ds(parts[0], hf)], hp.at[x, c, 0], 0)
     own_piece.wait()
 
@@ -171,6 +171,7 @@
             )
         rest_copy = bring(hz.at[rest, :, pl.ds(parts[0], hf)], hp.at[x, c, rest], 4 + 2 * NX)
         events.append((4.5, len(events), 2, 0, 1))
+    columns(1, 0, (2,))
     columns(1, 1)
     columns(0, 0)
     columns(0, 1)

time: 93 us -> 91.6 us (0.985)
  Pallas kernels: 90.3 us -> 89.1 us
    pallas_call x1, Pallas kernels: 90.3 us -> 89.1 us  [local(): pl.pallas_call(kernel, out_shape=jax.ShapeDtypeStruct((F, vd), bf16), in_...]
where the time goes in v4:
time: 91.6 us; the launch traced here: 91.4 us
  Pallas kernels  89.1 us (97%)
  local copies, waits for them, and re-layouts  2.26 us (2%)
    pallas_call x1, Pallas kernels, local(): pl.pallas_call(kernel, out_shape=jax.ShapeDtypeStruct((F, vd), bf16), in_...  89.1 us
    unnamed x1, local copies, waits for them, and re-layouts  2.26 us

profile of v4, /device:TPU:1, one launch (start us, length us, event | category | flops | bytes accessed | tf_op | source)
XLA Modules:
  0.0 91.4 jit_solution(5221525359969440857)
XLA Ops:
  0.0 89.1 %shard_map.55 = bf16[512,1024]{1,0:T(8,128)(2,1)} custom-call(bf16[2,256,1024]{2,1,0:T(8,128)(2,1)} %bitcast.4, bf16[2,256,1024]{2,1,0:T(8,128)(2,1)} %bitcast.5, bf16[2,256,1024]{2,1,0:T(8,128)(2,1)} %bitcast.6, bf16[8,512]{1,0:T(8,128)(2,1)} %hid.1, s32[1,512]{1,0:T(1,128)} %bitcast.7), custom_call_target="tpu_custom_call" | custom-call | tf_op jit(solution)/shard_map/pallas_call | solution.py:427
  89.1 2.3 %copy.7 = bf16[512,1024]{1,0:T(8,128)(2,1)} copy(bf16[512,1024]{1,0:T(8,128)(2,1)} %shard_map.55) | data formatting | bytes 2097152
